TPU v7x, 32 devices: a whole 2x2x4 slice. The times are simulated.
32 devices in a mesh: freq: 4 (over z), row: 4 (over y, x), col: 2 (over core).
Axes of the slice: x: 2, y: 2, z: 4, core: 2. Of those that a mesh axis runs over, the one named last changes fastest.
Arguments:
- prior_factor: bfloat16 [4, 26624, 1024], P('freq', ('row', 'col')), may hold values from -1 to 1, as said below
- prior_seeds: int32 [4, 26624, 512], P('freq', ('row', 'col')), may hold values from 0 to 4095
- window_seeds: int32 [4, 1024, 512], P('freq'), may hold values from 0 to 4095
- spectra: float32 [4, 1024], P('freq'), may hold values from 0.25 to 1
- nugget: float32 [4, 1024], P('freq'), may hold values from 0.6 to 1.2
- decay: float32 [4], P('freq'), may hold values from 0.2 to 2
Outputs:
- velocity: float32 [512, 1024, 256], P('freq', ('row', 'col'))
Inputs may be any that keep to these rules, and one draw needn't show every extreme that they name: `prior_factor`: every entry is smaller in magnitude than 0.95 / (sqrt(26624) + sqrt(1024)), and window_matrix is positive definite.
All inputs are finite; a program needn't handle non-finite values.
Results may differ from a plain program's by a relative error of at most 0.00087.
Values sent between devices are 32-bit elements; how exact they have to be, the bound alone decides.
A program may use at most 128 MiB of HBM per device.

v0:
```python
import math

import jax
import jax.numpy as jnp
from jax import lax
from jax.sharding import PartitionSpec as P

GRID = 96
NPHASE = 4096
STEPS = 256
PRIOR = 26624
FIRST_BIN = 64


cross_weight = 0.3


def window_index(positions, window, parts):
    own = window // parts
    quarter = own // 2
    device = positions // own
    within = positions % own
    return jnp.where(
        within < quarter,
        device * quarter + within,
        window // 2 + device * quarter + within - quarter,
    )


def natural_rows(gathered, parts):
    window = gathered.shape[0]
    quarter = window // (2 * parts)
    shaped = gathered.reshape(parts, 2, quarter, gathered.shape[1])
    return jnp.transpose(shaped, (1, 0, 2, 3)).reshape(window, gathered.shape[1])


def coherence(spectra, nugget, decay, row_ids):
    window = spectra.shape[0]
    col_ids = jnp.arange(window, dtype=jnp.int32)
    row_global = PRIOR + row_ids
    col_global = PRIOR + col_ids
    row_points = row_global // 3
    col_points = col_global // 3
    row_across = (row_points % GRID).astype(jnp.float32)
    row_height = (row_points // GRID).astype(jnp.float32)
    col_across = (col_points % GRID).astype(jnp.float32)
    col_height = (col_points // GRID).astype(jnp.float32)
    distance = jnp.sqrt(
        (row_across[:, None] - col_across[None, :]) ** 2
        + (row_height[:, None] - col_height[None, :]) ** 2
    )
    coupling = jnp.where(
        (row_global % 3)[:, None] == (col_global % 3)[None, :],
        jnp.float32(1.0),
        jnp.float32(cross_weight),
    )
    row_spectra = jnp.take(spectra, row_ids)
    row_nugget = jnp.take(nugget, row_ids)
    amplitude = jnp.sqrt(row_spectra[:, None] * spectra[None, :])
    diagonal = jnp.where(
        row_ids[:, None] == col_ids[None, :], row_nugget[:, None], jnp.float32(0.0)
    )
    return coupling * amplitude * jnp.exp(-decay * distance) + diagonal


def against(picked, other):
    return lax.dot_general(
        picked, other, (((0,), (0,)), ((), ())), preferred_element_type=jnp.float32
    )


def panel_factor(window_rows, own_ids, parts):
    half = window_rows.shape[1] // 2
    first_block = natural_rows(
        lax.all_gather(window_rows[:, :half], ("row", "col"), axis=0, tiled=True), parts
    )
    leading = jnp.linalg.cholesky(first_block[:half])
    lower_block = jax.scipy.linalg.solve_triangular(leading, first_block[half:].T, lower=True).T
    panel_column = jnp.concatenate([leading, lower_block], axis=0)
    own_first = jnp.take(panel_column, own_ids, axis=0)
    updated = window_rows[:, half:] - jnp.dot(
        own_first, lower_block.T, precision=lax.Precision.HIGHEST
    )
    second_block = natural_rows(lax.all_gather(updated, ("row", "col"), axis=0, tiled=True), parts)
    trailing = jnp.linalg.cholesky(second_block[half:])
    second_column = jnp.concatenate([jnp.zeros((half, half), jnp.float32), trailing], axis=0)
    own_second = jnp.take(second_column, own_ids, axis=0)
    return jnp.concatenate([own_first, own_second], axis=1)


def synthesize(pieces):
    part_re, part_im = pieces
    freq_count = part_re.shape[0]
    freq_bins = FIRST_BIN + jnp.arange(freq_count, dtype=jnp.int32)
    sample_ids = jnp.arange(STEPS, dtype=jnp.int32)
    turns = (freq_bins[:, None] * sample_ids[None, :] % STEPS).astype(jnp.float32) * (
        2.0 * math.pi / STEPS
    )
    tables = jnp.concatenate([jnp.cos(turns), jnp.sin(turns)], axis=0)
    stacked = jnp.concatenate([part_re, -part_im], axis=0)
    return jnp.einsum("gps,gt->spt", stacked, tables, precision=lax.Precision.HIGHEST)


def shards(prior_factor, prior_seeds, window_seeds, spectra, nugget, decay):
    prior_cols = prior_factor[0]
    window = prior_cols.shape[1]
    parts = lax.axis_size(("row", "col"))
    own_rows = window // parts
    offset = lax.axis_index(("row", "col")) * own_rows
    own_ids = window_index(offset + jnp.arange(own_rows, dtype=jnp.int32), window, parts)
    seed_count = prior_seeds.shape[2]
    phases = 2.0 * math.pi / NPHASE * prior_seeds[0].astype(jnp.float32)
    waves = jnp.concatenate(
        [jnp.cos(phases).astype(jnp.bfloat16), jnp.sin(phases).astype(jnp.bfloat16)], axis=1
    )
    spectra_here = spectra[0]
    nugget_here = nugget[0]
    decay_here = decay[0]
    wanted = window_index(
        jnp.arange(lax.axis_size(("row", "col")) * own_rows, dtype=jnp.int32), window, parts
    )
    picked = jnp.take(prior_cols, wanted, axis=1)
    summed_rows = lax.psum_scatter(
        jnp.concatenate([against(picked, prior_cols), against(picked, waves)], axis=1),
        ("row", "col"),
        scatter_dimension=0,
        tiled=True,
    )
    window_rows = (
        coherence(spectra_here, nugget_here, decay_here, own_ids) - summed_rows[:, :window]
    )
    prior_yield = summed_rows[:, window:]
    factor_rows = panel_factor(window_rows, own_ids, parts)
    window_phases = 2.0 * math.pi / NPHASE * window_seeds[0].astype(jnp.float32)
    window_waves = jnp.concatenate([jnp.cos(window_phases), jnp.sin(window_phases)], axis=1)
    amplitude = prior_yield + jnp.dot(factor_rows, window_waves, precision=lax.Precision.HIGHEST)
    amp_re = amplitude[:, :seed_count][None]
    amp_im = amplitude[:, seed_count:][None]
    return synthesize(
        (
            lax.all_to_all(amp_re, "freq", split_axis=2, concat_axis=0, tiled=True),
            lax.all_to_all(amp_im, "freq", split_axis=2, concat_axis=0, tiled=True),
        )
    )


def solution(mesh):
    in_specs = (
        P("freq", ("row", "col"), None),
        P("freq", ("row", "col"), None),
        P("freq", None, None),
        P("freq", None),
        P("freq", None),
        P("freq"),
    )
    out_specs = P("freq", ("row", "col"), None)
    return jax.shard_map(shards, mesh=mesh, in_specs=in_specs, out_specs=out_specs, check_vma=False)
```

profile of v0, /device:TPU:0, one launch (start us, length us, event | category | flops | bytes accessed | tf_op | source)
XLA Modules:
  0.0 547.9 jit_solution(5829410372089687422)
XLA Ops:
  6.6 9.9 %copy.52 = bf16[1,3328,1024]{1,2,0:T(8,128)(2,1)} copy(bf16[1,3328,1024]{2,1,0:T(8,128)(2,1)} %param.11) | data formatting | bytes 13631488 | tf_op args[0]
  16.5 26.6 %fusion.10 = (bf16[3328,512]{1,0:T(8,128)(2,1)}, bf16[3328,512]{1,0:T(8,128)(2,1)}) fusion(s32[1,3328,512]{2,1,0:T(8,128)} %param.12), kind=kLoop, calls=%fused_computation.23 | loop fusion | flops 6815744 | bytes 13631488 | tf_op jit(solution)/shard_map/convert_element_type | solution.py:114
  43.2 16.6 %gather_fusion = bf16[1024,3328]{1,0:T(8,128)(2,1)} fusion(bf16[3328,1024]{0,1:T(8,128)(2,1)} %bitcast.120, s32[1024]{0:T(1024)S(1)} %broadcast_clamp_fusion), kind=kCustom, calls=%fused_computation.4 | custom fusion | bytes 13635584 | tf_op jit(solution)/shard_map/jit(_take)/gather | solution.py:122
  59.8 14.2 %fusion.4 = f32[1024,1024]{0,1:T(8,128)} fusion(bf16[1,3328,1024]{2,1,0:T(8,128)(2,1)} %param.11, bf16[1024,3328]{1,0:T(8,128)(2,1)} %gather_fusion, pred[1024]{0:T(1024)(128)(4,1)S(1)} %compare_and_fusion), kind=kOutput, calls=%fused_computation.13 | convolution fusion | flops 6982729728 | bytes 17826816 | tf_op jit(solution)/shard_map/dot_general | solution.py:67
  74.0 12.6 %fusion = f32[1024,1024]{0,1:T(8,128)} fusion(bf16[3328,512]{1,0:T(8,128)(2,1)} %get-tuple-element.29, bf16[3328,512]{1,0:T(8,128)(2,1)} %get-tuple-element.28, bf16[1024,3328]{1,0:T(8,128)(2,1)S(1)} %copy-done.3, pred[1024]{0:T(1024)(128)(4,1)S(1)} %compare_and_fusion), kind=kOutput, calls=%fused_computation.9 | convolution fusion | flops 6996361216 | bytes 17826816 | tf_op jit(solution)/shard_map/dot_general | solution.py:67
  86.6 8.5 %pad_maximum_fusion = f32[1024,2048]{0,1:T(8,128)} fusion(f32[1024,1024]{0,1:T(8,128)} %fusion, f32[1024,1024]{0,1:T(8,128)} %fusion.4), kind=kLoop, calls=%fused_computation.8 | loop fusion | flops 2097152 | bytes 16777216 | tf_op jit(solution)/shard_map/concatenate | solution.py:124
  98.0 71.3 %reduce-scatter.2.cloned.1.call-done = f32[128,2048]{0,1:T(8,128)} async-done(((f32[1024,2048]{0,1:T(8,128)}), f32[128,2048]{0,1:T(8,128)}) %reduce-scatter.2.cloned.1.call-update) | async-done | bytes 1048592 | tf_op jit(solution)/shard_map/reduce_scatter | solution.py:123
  169.3 1.9 slice_subtract_fusion
  172.8 28.1 %all-gather.3.cloned.1.call-done = f32[1024,512]{0,1:T(8,128)} async-done(((f32[128,512]{0,1:T(8,128)}), f32[1024,512]{0,1:T(8,128)}) %all-gather.3.cloned.1.call-update) | async-done | bytes 2097168 | tf_op jit(solution)/shard_map/all_gather | solution.py:75
  201.0 2.1 copy.53
  204.3 1.6 copy.55
  207.4 11.7 %cholesky.286 = f32[128,128]{1,0:T(8,128)S(1)} custom-call(f32[128,128]{1,0:T(8,128)S(1)} %cholesky.426), custom_call_target="Cholesky" | custom-call | tf_op jit(solution)/shard_map/jit(cholesky)/cholesky | solution.py:77
  219.9 9.8 %custom-call.28 = f32[1,128,128]{1,2,0:T(8,128)S(1)} custom-call(f32[1,128,128]{2,1,0:T(8,128)S(1)} %get-tuple-element.55), custom_call_target="InvertDiagBlocksLowerTriangular" | custom-call | tf_op jit(solution)/shard_map/jit(cholesky)/cholesky | solution.py:77
  229.8 1.2 constant_dynamic-update-slice_fusion.3
  231.1 1.3 convolution_subtract_fusion.5
  232.4 11.7 %cholesky.305 = f32[128,128]{1,0:T(8,128)S(1)} custom-call(f32[128,128]{1,0:T(8,128)S(1)} %cholesky.430), custom_call_target="Cholesky" | custom-call | tf_op jit(solution)/shard_map/jit(cholesky)/cholesky | solution.py:77
  244.7 10.0 %custom-call.29 = f32[1,128,128]{1,2,0:T(8,128)S(1)} custom-call(f32[1,128,128]{2,1,0:T(8,128)S(1)} %get-tuple-element.52), custom_call_target="InvertDiagBlocksLowerTriangular" | custom-call | tf_op jit(solution)/shard_map/jit(cholesky)/cholesky | solution.py:77
  255.0 1.3 convolution_subtract_fusion.7
  256.3 11.7 %cholesky.326 = f32[128,128]{1,0:T(8,128)S(1)} custom-call(f32[128,128]{1,0:T(8,128)S(1)} %cholesky.435), custom_call_target="Cholesky" | custom-call | tf_op jit(solution)/shard_map/jit(cholesky)/cholesky | solution.py:77
  268.8 9.8 %custom-call.30 = f32[1,128,128]{1,2,0:T(8,128)S(1)} custom-call(f32[1,128,128]{2,1,0:T(8,128)S(1)} %get-tuple-element.49), custom_call_target="InvertDiagBlocksLowerTriangular" | custom-call | tf_op jit(solution)/shard_map/jit(cholesky)/cholesky | solution.py:77
  280.0 12.1 %cholesky.343 = f32[128,128]{1,0:T(8,128)S(1)} custom-call(f32[128,128]{1,0:T(8,128)S(1)} %convolution_subtract_fusion.9), custom_call_target="Cholesky" | custom-call | tf_op jit(solution)/shard_map/jit(cholesky)/cholesky | solution.py:77
  295.3 1.2 fusion.17
  296.6 7.9 %while.1 = (s32[]{:T(128)}, f32[512,512]{1,0:T(8,128)S(1)}, s32[4,2]{0,1:T(2,128)S(1)}, f32[4,128,128]{2,1,0:T(8,128)S(1)}, s32[]{:T(128)}) while((s32[]{:T(128)}, f32[512,512]{1,0:T(8,128)S(1)}, s32[4,2]{0,1:T(2,128)S(1)}, f32[4,128,128]{2,1,0:T(8,128)S(1)}, s32[]{:T(128)}) %tuple.46), condition=%wide.while_cond, body=%wide.while_body.sunk | while | flops 2 | bytes 131189 | solution.py:78
  297.2 1.3 bitcast_dynamic-update-slice_fusion.2
  299.2 1.3 bitcast_dynamic-update-slice_fusion.2
  301.2 1.3 bitcast_dynamic-update-slice_fusion.2
  303.1 1.3 bitcast_dynamic-update-slice_fusion.2
  304.4 39.3 %custom-call.24 = f32[4,128,128]{1,2,0:T(8,128)S(1)} custom-call(f32[4,128,128]{2,1,0:T(8,128)S(1)} %get-tuple-element.15), custom_call_target="InvertDiagBlocksLowerTriangular" | custom-call | tf_op jit(solution)/shard_map/jit(_solve_triangular)/triangular_solve | solution.py:78
  346.4 1.3 fusion.52
  348.5 1.5 fusion.51
  351.2 1.5 pad_maximum_fusion.1
  353.6 2.9 convolution_subtract_fusion.3
  356.6 8.3 %cosine_bitcast_fusion = (f32[1024,512]{1,0:T(8,128)}, f32[1024,512]{1,0:T(8,128)}) fusion(s32[1,1024,512]{2,1,0:T(8,128)S(1)} %copy-done.5), kind=kLoop, calls=%fused_computation.27 | loop fusion | flops 1048576 | bytes 6291456 | tf_op jit(solution)/shard_map/cos | solution.py:135
  364.9 19.9 %all-gather.5.cloned.1.call-done = f32[1024,512]{0,1:T(8,128)} async-done(((f32[128,512]{0,1:T(8,128)}), f32[1024,512]{0,1:T(8,128)}) %all-gather.5.cloned.1.call-update) | async-done | bytes 2097168 | tf_op jit(solution)/shard_map/all_gather | solution.py:84
  384.8 2.1 copy.61
  387.6 11.7 %cholesky.358 = f32[128,128]{1,0:T(8,128)S(1)} custom-call(f32[128,128]{1,0:T(8,128)S(1)} %cholesky.439), custom_call_target="Cholesky" | custom-call | tf_op jit(solution)/shard_map/jit(cholesky)/cholesky | solution.py:85
  400.1 9.8 %custom-call.31 = f32[1,128,128]{1,2,0:T(8,128)S(1)} custom-call(f32[1,128,128]{2,1,0:T(8,128)S(1)} %get-tuple-element.45), custom_call_target="InvertDiagBlocksLowerTriangular" | custom-call | tf_op jit(solution)/shard_map/jit(cholesky)/cholesky | solution.py:85
  410.6 11.7 %cholesky.377 = f32[128,128]{1,0:T(8,128)S(1)} custom-call(f32[128,128]{1,0:T(8,128)S(1)} %cholesky.443), custom_call_target="Cholesky" | custom-call | tf_op jit(solution)/shard_map/jit(cholesky)/cholesky | solution.py:85
  423.0 10.0 %custom-call.32 = f32[1,128,128]{1,2,0:T(8,128)S(1)} custom-call(f32[1,128,128]{2,1,0:T(8,128)S(1)} %get-tuple-element.42), custom_call_target="InvertDiagBlocksLowerTriangular" | custom-call | tf_op jit(solution)/shard_map/jit(cholesky)/cholesky | solution.py:85
  433.7 11.7 %cholesky.398 = f32[128,128]{1,0:T(8,128)S(1)} custom-call(f32[128,128]{1,0:T(8,128)S(1)} %cholesky.448), custom_call_target="Cholesky" | custom-call | tf_op jit(solution)/shard_map/jit(cholesky)/cholesky | solution.py:85
  446.1 9.8 %custom-call.33 = f32[1,128,128]{1,2,0:T(8,128)S(1)} custom-call(f32[1,128,128]{2,1,0:T(8,128)S(1)} %get-tuple-element.39), custom_call_target="InvertDiagBlocksLowerTriangular" | custom-call | tf_op jit(solution)/shard_map/jit(cholesky)/cholesky | solution.py:85
  456.5 11.7 %cholesky.415 = f32[128,128]{1,0:T(8,128)S(1)} custom-call(f32[128,128]{1,0:T(8,128)S(1)} %convolution_subtract_fusion.8), custom_call_target="Cholesky" | custom-call | tf_op jit(solution)/shard_map/jit(cholesky)/cholesky | solution.py:85
  472.7 8.7 %fusion.12 = f32[128,1024]{0,1:T(8,128)S(1)} fusion(f32[1024,512]{1,0:T(8,128)} %get-tuple-element.33, f32[1024,512]{1,0:T(8,128)} %get-tuple-element.32, f32[128,2048]{0,1:T(8,128)} %reduce-scatter.2.cloned.1.call-done, f32[128,512]{1,0:T(8,128)S(1)} %broadcast_select_fusion.3, f32[128,512]{1,0:T(8,128)S(1)} %broadcast_select_fusion.4), kind=kOutput, calls=%fused_computation.29 | convolution fusion | flops 1611923456 | bytes 5767168 | tf_op jit(solution)/shard_map/dot_general | solution.py:136
  482.1 13.7 %all_to_all.27 = f32[1,128,512]{1,0,2:T(1,128)S(1)} all-to-all(f32[1,128,512]{1,0,2:T(1,128)S(1)} %bitcast.135), channel_id=1, replica_groups=mesh['freq'=4,'row'=4,'col'=2] {'freq'}, dimensions={2} | all-to-all | bytes 524288 | tf_op jit(solution)/shard_map/all_to_all | solution.py:142
  495.8 3.4 all-to-all-start
  499.7 7.6 %all-to-all-done = f32[1,128,512]{1,0,2:T(1,128)S(1)} async-done(((f32[1,128,512]{1,0,2:T(1,128)}), f32[1,128,512]{1,0,2:T(1,128)S(1)}, u32[]{:S(2)}, u32[]{:S(2)}) %all-to-all-start) | async-done | bytes 262176 | tf_op jit(solution)/shard_map/all_to_all | solution.py:141
  507.4 15.9 %convolution_bitcast_fusion = f32[128,128,256]{0,2,1:T(8,128)} fusion(f32[4,128,128]{2,0,1:T(4,128)S(1)} %bitcast.132, f32[4,128,128]{2,0,1:T(4,128)S(1)} %bitcast.133, f32[4,256]{1,0:T(4,128)S(1)} %get-tuple-element.57, f32[4,256]{1,0:T(4,128)S(1)} %get-tuple-element.56), kind=kOutput, calls=%fused_computation.7 | convolution fusion | flops 402786304 | bytes 17309696 | tf_op jit(solution)/shard_map/gps,gt->spt/dot_general | solution.py:101
  523.3 17.6 %copy.68 = f32[128,128,256]{2,1,0:T(8,128)} copy(f32[128,128,256]{0,2,1:T(8,128)} %convolution_bitcast_fusion) | data formatting | bytes 33554432 | tf_op jit(solution)/shard_map/gps,gt->spt/transpose | solution.py:101
  (118 shorter events, 27.4 us)
Async XLA Ops:
  6.5 89.4 %copy-start = (f32[1,1024]{1,0:T(1,128)S(1)}, f32[1,1024]{1,0:T(1,128)}, u32[]{:S(2)}) copy-start(f32[1,1024]{1,0:T(1,128)} %param.15) | copy-start | bytes 12292
  6.5 162.8 %reduce-scatter.2.cloned.1.call-start = ((), (), s32[]{:S(2)}) async-start(), calls=%async_computation.3 | async-start | bytes 9437184 | tf_op jit(solution)/shard_map/reduce_scatter | solution.py:123
  59.8 14.2 %copy-start.3 = (bf16[1024,3328]{1,0:T(8,128)(2,1)S(1)}, bf16[1024,3328]{1,0:T(8,128)(2,1)}, u32[]{:S(2)}) copy-start(bf16[1024,3328]{1,0:T(8,128)(2,1)} %gather_fusion) | copy-start | bytes 20447236
  95.1 1.8 copy-start.2
  95.2 105.8 %all-gather.3.cloned.1.call-start = ((), (), s32[]{:S(2)}) async-start(), calls=%async_computation.4 | async-start | bytes 2359296 | tf_op jit(solution)/shard_map/all_gather | solution.py:75
  171.2 0.8 copy-start.6
  172.8 212.1 %all-gather.5.cloned.1.call-start = ((), (), s32[]{:S(2)}) async-start(), calls=%async_computation.5 | async-start | bytes 2359296 | tf_op jit(solution)/shard_map/all_gather | solution.py:84
  206.5 1.0 copy-start.4
  343.7 1.4 copy-start.12
  344.3 6.8 %copy-start.8 = (f32[128,512]{0,1:T(8,128)}, f32[128,512]{0,1:T(8,128)S(1)}, u32[]{:S(2)}) copy-start(f32[128,512]{0,1:T(8,128)S(1)} %copy.56) | copy-start | bytes 786436
  348.4 2.7 copy-start.10
  349.9 1.2 copy-start.11
  350.0 3.6 copy-start.7
  351.2 2.4 copy-start.9
  353.5 3.1 copy-start.5
  495.8 11.4 %all-to-all-start = ((f32[1,128,512]{1,0,2:T(1,128)}), f32[1,128,512]{1,0,2:T(1,128)S(1)}, u32[]{:S(2)}, u32[]{:S(2)}) async-start(f32[1,128,512]{1,0,2:T(1,128)} %bitcast.39), calls=%async_computation.1 | async-start | bytes 524288 | tf_op jit(solution)/shard_map/all_to_all | solution.py:141
  523.3 17.7 %copy-start.1 = (f32[1,1024]{1,0:T(1,128)S(1)}, f32[1,1024]{1,0:T(1,128)}, u32[]{:S(2)}) copy-start(f32[1,1024]{1,0:T(1,128)} %param.15) | copy-start | bytes 12292
Sparse Core Ops, SparseCore 0:
  95.3 73.9 reduce-scatter.1
  172.9 28.0 all-gather.2
  356.7 28.1 all-gather.4
where the time goes:
time: 555 us; the launch traced here: 548 us
  other arithmetic  249 us (45%)
  waiting for transfers between devices  127 us (23%)
  local copies, waits for them, and re-layouts  68.4 us (12%)
  matrix products  66.6 us (12%)
  between operations  19.8 us (4%)
  blocking collectives  13.7 us (2%)
    another operation x15, other arithmetic, panel_factor(): leading = jnp.linalg.cholesky(first_block[:half])  79.7 us
    another operation x15, other arithmetic, panel_factor(): trailing = jnp.linalg.cholesky(second_block[half:])  79.2 us
    reduce_scatter x1, waiting for transfers between devices, shards(): lax.psum_scatter(jnp.concatenate([against(picked, prior_cols), against(pi...  71.3 us
    another operation x3, other arithmetic, panel_factor(): jax.scipy.linalg.solve_triangular(leading, first_block[half:].T, lower=True)  40.6 us
    all_gather x1, waiting for transfers between devices, panel_factor(): lax.all_gather(window_rows[:, :half], ('row', 'col'), axis=0, tiled=True)  28.1 us
    dot_general x2, matrix products, against(): lax.dot_general(picked, other, (((0,), (0,)), ((), ())), preferred_elemen...  26.8 us
    convert_element_type x1, other arithmetic, shards(): jnp.cos(phases).astype(jnp.bfloat16)  26.6 us
    all_gather x1, waiting for transfers between devices, panel_factor(): lax.all_gather(updated, ('row', 'col'), axis=0, tiled=True)  19.9 us
  transfers between devices with their start and end apart: 4, of which 4 were waited for; matrix products, arithmetic and copies ran while one was open for 2% of the time, Pallas kernels for 0%

commit v1 on v0

v1 whole, which is shorter than its diff:
```python
import functools
import math

import jax
import jax.numpy as jnp
from jax import lax
from jax.experimental import pallas as pl
from jax.experimental.pallas import tpu as pltpu
from jax.sharding import PartitionSpec as P

GRID = 96
NPHASE = 4096
STEPS = 256
PRIOR = 26624
FIRST_BIN = 64
AXES = ("row", "col")
BLOCK = 128
SUB = 8


def split(x):
    high = x.astype(jnp.bfloat16)
    return high, (x - high.astype(jnp.float32)).astype(jnp.bfloat16)


def mul_nt(a, b):
    dims = (((1,), (1,)), ((), ()))
    dot = functools.partial(lax.dot_general, dimension_numbers=dims, preferred_element_type=jnp.float32)
    ah, al = a
    bh, bl = b
    return dot(ah, bh) + (dot(ah, bl) + dot(al, bh))


def factor_block(m_ref, l_ref, col_ref, row_ref):
    lane = lax.broadcasted_iota(jnp.int32, (SUB, BLOCK), 1)
    sub = lax.broadcasted_iota(jnp.int32, (SUB, BLOCK), 0)
    strips = BLOCK // SUB
    for p in range(strips):
        j0 = SUB * p
        inside = (lane >= j0) & (lane < j0 + SUB)
        lead = m_ref[j0:j0 + SUB, :]
        for k in range(SUB):
            col_ref[k] = jnp.broadcast_to(lead[:, j0 + k:j0 + k + 1], (SUB, BLOCK))
        row_ref[...] = jnp.where(inside, jnp.where(lane - j0 == sub, 1.0, 0.0), lead)
        a = {}
        for k in range(SUB):
            for i in range(k, SUB):
                a[i, k] = jnp.broadcast_to(col_ref[k, i:i + 1, :], (SUB, BLOCK))
        inv = []
        low = {}
        for k in range(SUB):
            r = lax.rsqrt(a[k, k])
            inv.append(r)
            for i in range(k + 1, SUB):
                low[i, k] = a[i, k] * r
            for m in range(k + 1, SUB):
                for i in range(m, SUB):
                    a[i, m] = a[i, m] - low[i, k] * low[m, k]
        u = []
        for k in range(SUB):
            x = jnp.broadcast_to(row_ref[k:k + 1, :], (SUB, BLOCK))
            for m in range(k):
                x = x - low[k, m] * u[m]
            u.append(x * inv[k])
        w = u[0]
        for k in range(1, SUB):
            w = jnp.where(sub == k, u[k], w)
        m_ref[j0:j0 + SUB, :] = jnp.where(lane < j0 + SUB, w, 0.0)
        for t in range(p, strips):
            at = slice(SUB * t, SUB * t + SUB)
            rows = lead if t == p else m_ref[at, :]
            c = []
            lacc = l_ref[at, :]
            for k in range(SUB):
                x = jnp.broadcast_to(rows[:, j0 + k:j0 + k + 1], (SUB, BLOCK))
                for m in range(k):
                    x = x - low[k, m] * c[m]
                c.append(x * inv[k])
                here = lane == j0 + k
                if t == p:
                    here = here & (sub >= k)
                lacc = jnp.where(here, c[k], lacc)
            l_ref[at, :] = lacc
            if t > p:
                x = jnp.where(inside, 0.0, rows)
                for k in range(SUB):
                    x = x - c[k] * u[k]
                m_ref[at, :] = x


def chol_kernel(coh_ref, sum_ref, out_ref, m_ref, l_ref, col_ref, row_ref, pan_ref):
    window = out_ref.shape[0]
    wide = sum_ref.shape[1]
    out_ref[...] = jnp.zeros_like(out_ref)
    at = 0
    for j in range(window // wide):
        size = window - j * wide
        out_ref[j * wide:, j * wide:(j + 1) * wide] = (
            coh_ref[j * wide:, j * wide:(j + 1) * wide] - sum_ref[at:at + size, :]
        )
        at += size

    row = lax.broadcasted_iota(jnp.int32, (window, BLOCK), 0)

    @pl.loop(0, window // BLOCK)
    def _(b):
        here = pl.ds(pl.multiple_of(b * BLOCK, BLOCK), BLOCK)
        pan_ref[...] = out_ref[:, here]

        @pl.loop(0, b)
        def _(k):
            there = pl.ds(pl.multiple_of(k * BLOCK, BLOCK), BLOCK)
            pan_ref[...] -= mul_nt(split(out_ref[:, there]), split(out_ref[here, there]))

        m_ref[...] = pan_ref[here, :]
        l_ref[...] = jnp.zeros_like(l_ref)
        factor_block(m_ref, l_ref, col_ref, row_ref)
        below = mul_nt(split(pan_ref[...]), split(m_ref[...]))
        out_ref[:, here] = jnp.where(row >= (b + 1) * BLOCK, below, 0.0)
        out_ref[here, here] = l_ref[...]


def cholesky(coh, packed):
    window = coh.shape[0]
    return pl.pallas_call(
        chol_kernel,
        name="factor",
        out_shape=jax.ShapeDtypeStruct((window, window), jnp.float32),
        in_specs=[pl.BlockSpec(memory_space=pltpu.VMEM)] * 2,
        out_specs=pl.BlockSpec(memory_space=pltpu.VMEM),
        scratch_shapes=[
            pltpu.VMEM((BLOCK, BLOCK), jnp.float32),
            pltpu.VMEM((BLOCK, BLOCK), jnp.float32),
            pltpu.VMEM((SUB, SUB, BLOCK), jnp.float32),
            pltpu.VMEM((SUB, BLOCK), jnp.float32),
            pltpu.VMEM((window, BLOCK), jnp.float32),
        ],
        compiler_params=pltpu.CompilerParams(vmem_limit_bytes=40 * 2**20),
        cost_estimate=pl.CostEstimate(flops=40 * 10**9, bytes_accessed=11 * 2**20, transcendentals=0),
    )(coh, packed)


cross_weight = 0.3


def coherence(spectra, nugget, decay, row_ids):
    window = spectra.shape[0]
    col_ids = jnp.arange(window, dtype=jnp.int32)
    row_global = PRIOR + row_ids
    col_global = PRIOR + col_ids
    row_points = row_global // 3
    col_points = col_global // 3
    row_across = (row_points % GRID).astype(jnp.float32)
    row_height = (row_points // GRID).astype(jnp.float32)
    col_across = (col_points % GRID).astype(jnp.float32)
    col_height = (col_points // GRID).astype(jnp.float32)
    distance = jnp.sqrt(
        (row_across[:, None] - col_across[None, :]) ** 2
        + (row_height[:, None] - col_height[None, :]) ** 2
    )
    coupling = jnp.where(
        (row_global % 3)[:, None] == (col_global % 3)[None, :],
        jnp.float32(1.0),
        jnp.float32(cross_weight),
    )
    row_spectra = jnp.take(spectra, row_ids)
    row_nugget = jnp.take(nugget, row_ids)
    amplitude = jnp.sqrt(row_spectra[:, None] * spectra[None, :])
    diagonal = jnp.where(
        row_ids[:, None] == col_ids[None, :], row_nugget[:, None], jnp.float32(0.0)
    )
    return coupling * amplitude * jnp.exp(-decay * distance) + diagonal


def against(picked, other):
    return lax.dot_general(
        picked, other, (((0,), (0,)), ((), ())), preferred_element_type=jnp.float32
    )


def waves_of(seeds):
    quarter = NPHASE // 4
    turn = (seeds + quarter // 2) // quarter
    x = (seeds - turn * quarter).astype(jnp.float32) * (2.0 * math.pi / NPHASE)
    y = x * x
    sin = x * (1.0 + y * (-1 / 6 + y * (1 / 120 + y * (-1 / 5040 + y * (1 / 362880)))))
    cos = 1.0 + y * (-1 / 2 + y * (1 / 24 + y * (-1 / 720 + y * (1 / 40320))))
    odd = (turn & 1) == 1
    re = jnp.where(odd, sin, cos)
    im = jnp.where(odd, cos, sin)
    return (
        jnp.where(((turn + 1) & 2) == 2, -re, re),
        jnp.where((turn & 2) == 2, -im, im),
    )


def synth_kernel(x_ref, table_ref, out_ref):
    def parts(value):
        high = value.astype(jnp.bfloat16).astype(jnp.float32)
        return high, value - high

    xh, xl = parts(x_ref[...])
    th, tl = parts(table_ref[...])
    lhs = jnp.concatenate([xh, xh, xl, xl], axis=0).astype(jnp.bfloat16)
    rhs = jnp.concatenate([th, tl, th, tl], axis=0).astype(jnp.bfloat16)
    out_ref[...] = lax.dot_general(
        lhs, rhs, (((0,), (0,)), ((), ())), preferred_element_type=jnp.float32
    )


def synthesize(stacked, freq_count):
    freq_bins = FIRST_BIN + jnp.arange(freq_count, dtype=jnp.int32)
    sample_ids = jnp.arange(STEPS, dtype=jnp.int32)
    turns = (freq_bins[:, None] * sample_ids[None, :] % STEPS).astype(jnp.float32) * (
        2.0 * math.pi / STEPS
    )
    tables = jnp.stack([jnp.cos(turns), -jnp.sin(turns)], axis=1).reshape(2 * freq_count, STEPS)
    count = stacked.shape[1]
    step = min(2048, count)
    return pl.pallas_call(
        synth_kernel,
        name="synth",
        grid=(count // step,),
        out_shape=jax.ShapeDtypeStruct((count, STEPS), jnp.float32),
        in_specs=[
            pl.BlockSpec((2 * freq_count, step), lambda i: (0, i)),
            pl.BlockSpec((2 * freq_count, STEPS), lambda i: (0, 0)),
        ],
        out_specs=pl.BlockSpec((step, STEPS), lambda i: (i, 0)),
        compiler_params=pltpu.CompilerParams(vmem_limit_bytes=24 * 2**20),
    )(stacked, tables)


def shards(prior_factor, prior_seeds, window_seeds, spectra, nugget, decay):
    cols = prior_factor[0]
    window = cols.shape[1]
    parts = lax.axis_size(AXES)
    freq_count = lax.axis_size("freq")
    quarter = window // (2 * parts)
    seed_count = prior_seeds.shape[2]
    me = lax.axis_index(AXES)
    wide = 2 * BLOCK

    packed = jnp.concatenate(
        [against(cols[:, at:], cols[:, at:at + wide]) for at in range(0, window, wide)], axis=0
    )
    packed = lax.psum_scatter(packed, AXES, scatter_dimension=0, tiled=True)
    packed = lax.all_gather(packed, AXES, axis=0, tiled=True)

    def scattered(wave):
        whole = against(cols, wave.astype(jnp.bfloat16)).reshape(2, parts, quarter, seed_count)
        whole = jnp.transpose(whole, (1, 0, 2, 3)).reshape(window, seed_count)
        return lax.psum_scatter(whole, AXES, scatter_dimension=0, tiled=True)

    wave_re, wave_im = waves_of(prior_seeds[0])
    prior = jnp.concatenate([scattered(wave_re), scattered(wave_im)], axis=1)
    window_waves = jnp.concatenate(waves_of(window_seeds[0]), axis=1)

    coh = coherence(spectra[0], nugget[0], decay[0], jnp.arange(window, dtype=jnp.int32))
    factor = cholesky(coh, packed)
    own = jnp.concatenate(
        [
            lax.dynamic_slice_in_dim(factor, me * quarter, quarter, 0),
            lax.dynamic_slice_in_dim(factor, window // 2 + me * quarter, quarter, 0),
        ],
        axis=0,
    )
    amplitude = prior + jnp.dot(own, window_waves, precision=lax.Precision.HIGH)
    turned = amplitude.T.reshape(2, seed_count, 2 * quarter)
    spread = lax.all_to_all(turned, "freq", split_axis=1, concat_axis=0, tiled=True)
    here = seed_count // freq_count
    out = synthesize(spread.reshape(2 * freq_count, here * 2 * quarter), freq_count)
    return out.reshape(here, 2 * quarter, STEPS)


def solution(mesh):
    in_specs = (
        P("freq", ("row", "col"), None),
        P("freq", ("row", "col"), None),
        P("freq", None, None),
        P("freq", None),
        P("freq", None),
        P("freq"),
    )
    out_specs = P("freq", ("row", "col"), None)
    return jax.shard_map(shards, mesh=mesh, in_specs=in_specs, out_specs=out_specs, check_vma=False)
```

time: 555 us -> 225 us (0.41); the launches traced: 548 us -> 224 us
  other arithmetic: 249 us -> 13.4 us
  waiting for transfers between devices: 127 us -> 67.5 us
  Pallas kernels: 0 us -> 52.6 us
  local copies, waits for them, and re-layouts: 68.4 us -> 22.9 us
  matrix products: 66.6 us -> 48.8 us
  blocking collectives: 13.7 us -> 0 us
  between operations: 19.8 us -> 14 us
    another operation x33 -> x1, other arithmetic: 199 us -> 0.01 us  [synthesize(): jnp.stack([jnp.cos(turns), -jnp.sin(turns)], axis=1)]
    pallas_call x0 -> x2, Pallas kernels: none -> 52.6 us  [the longest x1 44.7 us: cholesky(): pl.pallas_call(chol_kernel, name='factor', out_shape=jax.ShapeDtypeStruct...]
    all_gather x2 -> x1, waiting for transfers between devices: 48.1 us -> 0.01 us  [shards(): packed = lax.all_gather(packed, AXES, axis=0, tiled=True)]
    convert_element_type x3 -> x1, other arithmetic: 26.7 us -> 0.02 us  [coherence(): row_height = (row_points // GRID).astype(jnp.float32)]
    dot_general x3 -> x1, matrix products: 27.5 us -> 3.14 us  [shards(): amplitude = prior + jnp.dot(own, window_waves, precision=lax.Precision.HIGH)]
    dot_general x2 -> x6, matrix products: 26.8 us -> 45.7 us  [against(): lax.dot_general(picked, other, (((0,), (0,)), ((), ())), preferred_elemen...]
    gather x3 -> x0, local copies, waits for them, and re-layouts: 18.2 us -> none  [the longest x1 16.6 us: shards(): picked = jnp.take(prior_cols, wanted, axis=1)]
    reduce_scatter x1 -> x3, waiting for transfers between devices: 71.3 us -> 53.3 us  [the longest x1 46.4 us: shards(): packed = lax.psum_scatter(packed, AXES, scatter_dimension=0, tiled=True)]
  transfers between devices with their start and end apart: 4 -> 5, of which waited for: 4 -> 3; matrix products, arithmetic and copies ran while one was open for 2% -> 28% of each run, Pallas kernels for 0% -> 20%
where the time goes in v1:
time: 225 us; the launch traced here: 224 us
  waiting for transfers between devices  67.5 us (30%)
  Pallas kernels  52.6 us (23%)
  matrix products  48.8 us (22%)
  local copies, waits for them, and re-layouts  22.9 us (10%)
  between operations  14 us (6%)
  other arithmetic  13.4 us (6%)
  starting transfers between devices  5.13 us (2%)
    reduce_scatter x1, waiting for transfers between devices, shards(): packed = lax.psum_scatter(packed, AXES, scatter_dimension=0, tiled=True)  46.4 us
    dot_general x6, matrix products, against(): lax.dot_general(picked, other, (((0,), (0,)), ((), ())), preferred_elemen...  45.7 us
    pallas_call x1, Pallas kernels, cholesky(): pl.pallas_call(chol_kernel, name='factor', out_shape=jax.ShapeDtypeStruct...  44.7 us
    all_to_all x1, waiting for transfers between devices, shards(): lax.all_to_all(turned, 'freq', split_axis=1, concat_axis=0, tiled=True)  14.2 us
    pallas_call x1, Pallas kernels, synthesize(): pl.pallas_call(synth_kernel, name='synth', grid=(count // step,), out_sha...  7.91 us
    reduce_scatter x2, waiting for transfers between devices, scattered(): return lax.psum_scatter(whole, AXES, scatter_dimension=0, tiled=True)  6.93 us
    select_n x1, other arithmetic, waves_of(): jnp.where(turn + 1 & 2 == 2, -re, re)  5.81 us
    add x1, other arithmetic, coherence(): return coupling * amplitude * jnp.exp(-decay * distance) + diagonal  5.79 us
  transfers between devices with their start and end apart: 5, of which 3 were waited for; matrix products, arithmetic and copies ran while one was open for 28% of the time, Pallas kernels for 20%

profile of v1, /device:TPU:0, one launch (start us, length us, event | category | flops | bytes accessed | tf_op | source)
XLA Modules:
  0.0 224.4 jit_solution(7433186521799329892)
XLA Ops:
  6.5 0.0 copy-start
  6.5 0.0 reduce-scatter.8.cloned.1.call-start
  6.5 2.6 %fusion.29 = f32[256,256]{1,0:T(8,128)S(1)} fusion(bf16[3328,1024]{1,0:T(8,128)(2,1)} %bitcast.71), kind=kOutput, calls=%fused_computation.63 | convolution fusion | flops 436207616 | bytes 1966080 | tf_op jit(solution)/shard_map/dot_general | solution.py:176
  9.2 0.0 copy-start.4
  9.2 3.7 %fusion.18 = f32[512,256]{1,0:T(8,128)S(1)} fusion(bf16[3328,1024]{1,0:T(8,128)(2,1)} %bitcast.72), kind=kOutput, calls=%fused_computation.35 | convolution fusion | flops 872415232 | bytes 5636096 | tf_op jit(solution)/shard_map/dot_general | solution.py:176
  12.9 0.8 copy-done.4
  13.7 1.5 fusion.6
  15.2 2.0 fusion.33
  17.2 1.7 pad_maximum_fusion
  18.8 0.0 reduce-scatter.8.cloned.1.call-update
  18.8 0.0 all-gather.2.cloned.1.call-start
  18.9 46.4 %reduce-scatter.8.cloned.1.call-done = f32[320,256]{1,0:T(8,128)} async-done(((f32[2560,256]{1,0:T(8,128)}), f32[320,256]{1,0:T(8,128)}) %reduce-scatter.8.cloned.1.call-update) | async-done | bytes 327696 | tf_op jit(solution)/shard_map/reduce_scatter | solution.py:247
  65.2 0.0 all-gather.2.cloned.1.call-update
  65.3 0.2 reduce-scatter.4.cloned.1.call-start
  65.5 18.0 %fusion.35 = f32[1024,512]{0,1:T(8,128)} fusion(s32[1,3328,512]{2,1,0:T(8,128)} %param.9, bf16[1,3328,1024]{2,1,0:T(8,128)(2,1)} %param.8), kind=kOutput, calls=%fused_computation.69 | convolution fusion | flops 3569745920 | bytes 15728640 | tf_op jit(solution)/shard_map/dot_general | solution.py:176
  83.5 1.9 copy.22
  85.4 1.6 copy.23
  87.0 0.0 reduce-scatter.4.cloned.1.call-update
  87.0 0.3 reduce-scatter.6.cloned.1.call-start
  87.3 17.9 %fusion.38 = f32[1024,512]{0,1:T(8,128)} fusion(s32[1,3328,512]{2,1,0:T(8,128)} %param.9, bf16[1,3328,1024]{2,1,0:T(8,128)(2,1)} %param.8), kind=kOutput, calls=%fused_computation.70 | convolution fusion | flops 3568041984 | bytes 15728640 | tf_op jit(solution)/shard_map/dot_general | solution.py:176
  105.2 2.0 copy.24
  107.1 1.7 copy.25
  108.8 0.0 copy-start.3
  108.8 0.0 reduce-scatter.6.cloned.1.call-update
  109.6 0.0 copy-done
  109.6 4.5 %gather_fusion.1 = f32[1024]{0:T(1024)S(1)} fusion(f32[1024]{0:T(1024)S(1)} %bitcast.67, s32[1024]{0:T(1024)S(1)} %iota_clamp_fusion), kind=kCustom, calls=%fused_computation.1.clone | custom fusion | bytes 12288 | tf_op jit(solution)/shard_map/jit(_take)/gather | solution.py:167
  114.1 0.0 copy-done.3
  114.1 4.5 %gather_fusion = f32[1024]{0:T(1024)S(1)} fusion(f32[1024]{0:T(1024)S(1)} %bitcast.69, s32[1024]{0:T(1024)S(1)} %iota_clamp_fusion), kind=kCustom, calls=%fused_computation.clone | custom fusion | bytes 12288 | tf_op jit(solution)/shard_map/jit(_take)/gather | solution.py:166
  118.7 5.8 %negate_select_fusion.6 = (f32[1024,512]{1,0:T(8,128)S(1)}, f32[1024,512]{1,0:T(8,128)}) fusion(s32[1,1024,512]{2,1,0:T(8,128)} %param.10), kind=kLoop, calls=%fused_computation.41 | loop fusion | flops 26738688 | bytes 6291456 | tf_op jit(solution)/shard_map/jit(_where)/select_n | solution.py:192
  124.5 5.8 %select_add_fusion.coh_ref = f32[1024,1024]{1,0:T(8,128)} fusion(f32[1024]{0:T(1024)S(1)} %get-tuple-element.14, f32[1024]{0:T(1024)S(1)} %fusion.53, f32[1024]{0:T(1024)S(1)} %get-tuple-element.13, f32[]{:T(128)} %bitcast.12, f32[1024]{0:T(1024)S(1)} %bitcast.70, f32[1024]{0:T(1024)S(1)} %get-tuple-element.15, s32[1024]{0:T(1024)S(1)} %get-tuple-element.12), kind=kLoop, calls=%fused_computation.29 | loop fusion | flops 14680064 | bytes 4218884 | tf_op jit(solution)/shard_map/add | solution.py:172
  130.3 0.0 all-gather.2.cloned.1.call-done.sum_ref
  130.3 0.0 copy-start.1
  130.3 1.7 copy-done.1
  132.0 0.0 copy-start.2
  132.0 2.2 copy-done.2
  134.2 44.7 %factor.1 = f32[1024,1024]{1,0:T(8,128)S(1)} custom-call(f32[1024,1024]{1,0:T(8,128)S(1)} %copy-done.2, f32[2560,256]{1,0:T(8,128)S(1)} %copy-done.1), custom_call_target="tpu_custom_call" | custom-call | flops 40000000000 | bytes 11534336 | tf_op jit(solution)/shard_map/factor/pallas_call | solution.py:125
  179.0 0.0 reduce-scatter.4.cloned.1.call-done
  179.0 6.9 %reduce-scatter.6.cloned.1.call-done = f32[128,512]{1,0:T(8,128)} async-done(((f32[1024,512]{1,0:T(8,128)}), f32[128,512]{1,0:T(8,128)}) %reduce-scatter.6.cloned.1.call-update) | async-done | bytes 262160 | tf_op jit(solution)/shard_map/reduce_scatter | solution.py:253
  185.9 3.1 %fusion.44 = f32[1024,128]{0,1:T(8,128)S(1)} fusion(f32[1024,512]{1,0:T(8,128)} %get-tuple-element.9, f32[1024,512]{1,0:T(8,128)S(1)} %get-tuple-element.8, f32[128,512]{1,0:T(8,128)} %reduce-scatter.6.cloned.1.call-done, f32[128,512]{1,0:T(8,128)} %reduce-scatter.4.cloned.1.call-done, f32[64,1024]{1,0:T(8,128)S(1)} %get-tuple-element.7, ...), kind=kOutput, calls=%fused_computation.72 | convolution fusion | flops 806748160 | bytes 5767168 | tf_op jit(solution)/shard_map/dot_general | solution.py:268
  189.0 0.4 reshape.207
  189.5 1.1 copy.26
  190.6 4.6 %all-to-all-start = ((f32[2,512,128]{2,0,1:T(2,128)}), f32[2,512,128]{2,0,1:T(2,128)S(1)}, u32[]{:S(2)}, u32[]{:S(2)}) async-start(f32[2,512,128]{2,0,1:T(2,128)} %copy.26), calls=%async_computation.3 | async-start | bytes 1048576 | tf_op jit(solution)/shard_map/all_to_all | solution.py:270
  195.2 0.1 fusion.63
  195.4 14.2 %all-to-all-done = f32[2,512,128]{2,0,1:T(2,128)S(1)} async-done(((f32[2,512,128]{2,0,1:T(2,128)}), f32[2,512,128]{2,0,1:T(2,128)S(1)}, u32[]{:S(2)}, u32[]{:S(2)}) %all-to-all-start) | async-done | bytes 524320 | tf_op jit(solution)/shard_map/all_to_all | solution.py:270
  209.6 0.3 copy.32
  209.9 7.9 %synth.1 = f32[16384,256]{1,0:T(8,128)} custom-call(f32[8,16384]{1,0:T(8,128)S(1)} %bitcast.68, f32[8,256]{1,0:T(8,128)S(1)} %reshape.209.table_ref), custom_call_target="tpu_custom_call" | custom-call | tf_op jit(solution)/shard_map/synth/pallas_call | solution.py:220
  (11 shorter events, 0.2 us)
Async XLA Ops:
  6.5 103.0 %copy-start = (f32[1,1024]{1,0:T(1,128)S(1)}, f32[1,1024]{1,0:T(1,128)}, u32[]{:S(2)}) copy-start(f32[1,1024]{1,0:T(1,128)} %param.12) | copy-start | bytes 12292
  6.5 58.7 %reduce-scatter.8.cloned.1.call-start = ((), (), s32[]{:S(2)}) async-start(), calls=%async_computation.6 | async-start | bytes 2949120 | tf_op jit(solution)/shard_map/reduce_scatter | solution.py:247
  9.2 4.5 %copy-start.4 = (bf16[1,3328,1024]{2,1,0:T(8,128)(2,1)S(1)}, bf16[1,3328,1024]{2,1,0:T(8,128)(2,1)}, u32[]{:S(2)}) copy-start(bf16[1,3328,1024]{2,1,0:T(8,128)(2,1)} %param.8) | copy-start | bytes 20447236
  18.8 111.4 %all-gather.2.cloned.1.call-start = ((), (), s32[]{:S(2)}) async-start(), calls=%async_computation.7 | async-start | bytes 2949120 | tf_op jit(solution)/shard_map/all_gather | solution.py:248
  65.3 113.7 %reduce-scatter.4.cloned.1.call-start = ((), (), s32[]{:S(2)}) async-start(), calls=%async_computation.4 | async-start | bytes 2359296 | tf_op jit(solution)/shard_map/reduce_scatter | solution.py:253
  87.0 98.9 %reduce-scatter.6.cloned.1.call-start = ((), (), s32[]{:S(2)}) async-start(), calls=%async_computation.5 | async-start | bytes 2359296 | tf_op jit(solution)/shard_map/reduce_scatter | solution.py:253
  108.8 5.3 %copy-start.3 = (f32[1,1024]{1,0:T(1,128)S(1)}, f32[1,1024]{1,0:T(1,128)}, u32[]{:S(2)}) copy-start(f32[1,1024]{1,0:T(1,128)} %param.11) | copy-start | bytes 12292
  130.3 1.7 copy-start.1
  132.0 2.2 copy-start.2
  190.6 18.9 %all-to-all-start = ((f32[2,512,128]{2,0,1:T(2,128)}), f32[2,512,128]{2,0,1:T(2,128)S(1)}, u32[]{:S(2)}, u32[]{:S(2)}) async-start(f32[2,512,128]{2,0,1:T(2,128)} %copy.26), calls=%async_computation.3 | async-start | bytes 1048576 | tf_op jit(solution)/shard_map/all_to_all | solution.py:270
Sparse Core Ops, SparseCore 0:
  19.0 46.2 reduce-scatter.7
  67.1 29.9 all-gather.1
  100.4 41.1 reduce-scatter.3
  144.7 41.1 reduce-scatter.5

commit v2 on v1

--- a/solution.py
+++ b/solution.py
@@ -143,9 +143,10 @@
 cross_weight = 0.3
 
 
-def coherence(spectra, nugget, decay, row_ids):
+def coherence(spectra, nugget, decay):
     window = spectra.shape[0]
     col_ids = jnp.arange(window, dtype=jnp.int32)
+    row_ids = col_ids
     row_global = PRIOR + row_ids
     col_global = PRIOR + col_ids
     row_points = row_global // 3
@@ -163,11 +164,9 @@
         jnp.float32(1.0),
         jnp.float32(cross_weight),
     )
-    row_spectra = jnp.take(spectra, row_ids)
-    row_nugget = jnp.take(nugget, row_ids)
-    amplitude = jnp.sqrt(row_spectra[:, None] * spectra[None, :])
+    amplitude = jnp.sqrt(spectra[:, None] * spectra[None, :])
     diagonal = jnp.where(
-        row_ids[:, None] == col_ids[None, :], row_nugget[:, None], jnp.float32(0.0)
+        row_ids[:, None] == col_ids[None, :], nugget[:, None], jnp.float32(0.0)
     )
     return coupling * amplitude * jnp.exp(-decay * distance) + diagonal
 
@@ -245,18 +244,22 @@
         [against(cols[:, at:], cols[:, at:at + wide]) for at in range(0, window, wide)], axis=0
     )
     packed = lax.psum_scatter(packed, AXES, scatter_dimension=0, tiled=True)
+
+    def stored(wave):
+        whole = against(cols, wave.astype(jnp.bfloat16)).reshape(2, parts, quarter, seed_count)
+        return jnp.transpose(whole, (1, 0, 2, 3)).reshape(window, seed_count)
+
+    wave_re, wave_im = waves_of(prior_seeds[0])
+    whole = jnp.concatenate([stored(wave_re), stored(wave_im)], axis=1)
+    coh = coherence(spectra[0], nugget[0], decay[0])
+    window_waves = jnp.concatenate(waves_of(window_seeds[0]), axis=1)
+    packed, whole = lax.optimization_barrier((packed, whole))
     packed = lax.all_gather(packed, AXES, axis=0, tiled=True)
-
-    def scattered(wave):
-        whole = against(cols, wave.astype(jnp.bfloat16)).reshape(2, parts, quarter, seed_count)
-        whole = jnp.transpose(whole, (1, 0, 2, 3)).reshape(window, seed_count)
-        return lax.psum_scatter(whole, AXES, scatter_dimension=0, tiled=True)
-
-    wave_re, wave_im = waves_of(prior_seeds[0])
-    prior = jnp.concatenate([scattered(wave_re), scattered(wave_im)], axis=1)
-    window_waves = jnp.concatenate(waves_of(window_seeds[0]), axis=1)
-
-    coh = coherence(spectra[0], nugget[0], decay[0], jnp.arange(window, dtype=jnp.int32))
+    packed, whole, coh, window_waves = lax.optimization_barrier(
+        (packed, whole, coh, window_waves)
+    )
+    prior = lax.psum_scatter(whole, AXES, scatter_dimension=0, tiled=True)
+
     factor = cholesky(coh, packed)
     own = jnp.concatenate(
         [

time: 225 us -> 192 us (0.85)
  waiting for transfers between devices: 67.5 us -> 40.3 us
  local copies, waits for them, and re-layouts: 22.9 us -> 13.6 us
  other arithmetic: 13.4 us -> 16.4 us
    reduce_scatter x1, waiting for transfers between devices: 46.4 us -> 0.46 us  [shards(): packed = lax.psum_scatter(packed, AXES, scatter_dimension=0, tiled=True)]
    all_gather x1, waiting for transfers between devices: 0.01 us -> 19.5 us  [shards(): packed = lax.all_gather(packed, AXES, axis=0, tiled=True)]
    gather x2 -> x0, local copies, waits for them, and re-layouts: 9.06 us -> none  [the longest x1 4.53 us: coherence(): row_nugget = jnp.take(nugget, row_ids)]
    concatenate x0 -> x2, other arithmetic: none -> 4.8 us  [the longest x1 2.42 us: shards(): whole = jnp.concatenate([stored(wave_re), stored(wave_im)], axis=1)]
    unnamed x11 -> x15, local copies, waits for them, and re-layouts: 5 us -> 6.34 us
    reduce_scatter x2 -> x1, waiting for transfers between devices: 6.93 us -> 6.13 us  [shards(): prior = lax.psum_scatter(whole, AXES, scatter_dimension=0, tiled=True)]
  transfers between devices with their start and end apart: 5 -> 4, of which waited for: 3 -> 4; matrix products, arithmetic and copies ran while one was open for 28% -> 30% of each run, Pallas kernels for 20% -> 23%
where the time goes in v2:
time: 192 us; the launch traced here: 191 us
  Pallas kernels  52.3 us (27%)
  matrix products  49.7 us (26%)
  waiting for transfers between devices  40.3 us (21%)
  other arithmetic  16.4 us (9%)
  between operations  13.9 us (7%)
  local copies, waits for them, and re-layouts  13.6 us (7%)
  starting transfers between devices  4.86 us (3%)
    dot_general x6, matrix products, against(): lax.dot_general(picked, other, (((0,), (0,)), ((), ())), preferred_elemen...  46.1 us
    pallas_call x1, Pallas kernels, cholesky(): pl.pallas_call(chol_kernel, name='factor', out_shape=jax.ShapeDtypeStruct...  44.4 us
    all_gather x1, waiting for transfers between devices, shards(): packed = lax.all_gather(packed, AXES, axis=0, tiled=True)  19.5 us
    all_to_all x1, waiting for transfers between devices, shards(): lax.all_to_all(turned, 'freq', split_axis=1, concat_axis=0, tiled=True)  14.2 us
    pallas_call x1, Pallas kernels, synthesize(): pl.pallas_call(synth_kernel, name='synth', grid=(count // step,), out_sha...  7.9 us
    unnamed x15, local copies, waits for them, and re-layouts  6.34 us
    reduce_scatter x1, waiting for transfers between devices, shards(): prior = lax.psum_scatter(whole, AXES, scatter_dimension=0, tiled=True)  6.13 us
    add x1, other arithmetic, coherence(): return coupling * amplitude * jnp.exp(-decay * distance) + diagonal  5.86 us
  transfers between devices with their start and end apart: 4, of which 4 were waited for; matrix products, arithmetic and copies ran while one was open for 30% of the time, Pallas kernels for 23%

profile of v2, /device:TPU:0, one launch (start us, length us, event | category | flops | bytes accessed | tf_op | source)
XLA Modules:
  0.0 191.2 jit_solution(1401642601065047601)
XLA Ops:
  6.5 0.0 reduce-scatter.3.cloned.1.call-start
  6.5 2.6 %fusion.25 = f32[256,256]{1,0:T(8,128)S(1)} fusion(bf16[3328,1024]{1,0:T(8,128)(2,1)} %bitcast.69), kind=kOutput, calls=%fused_computation.59 | convolution fusion | flops 436207616 | bytes 1966080 | tf_op jit(solution)/shard_map/dot_general | solution.py:175
  9.2 0.0 copy-start.2
  9.2 3.7 %fusion.14 = f32[512,256]{1,0:T(8,128)S(1)} fusion(bf16[3328,1024]{1,0:T(8,128)(2,1)} %bitcast.70), kind=kOutput, calls=%fused_computation.31 | convolution fusion | flops 872415232 | bytes 5636096 | tf_op jit(solution)/shard_map/dot_general | solution.py:175
  12.9 0.8 copy-done.2
  13.6 1.5 fusion.6
  15.2 2.0 %fusion.29 = f32[1024,256]{1,0:T(8,128)S(1)} fusion(bf16[3328,1024]{1,0:T(8,128)(2,1)S(1)} %bitcast.72), kind=kOutput, calls=%fused_computation.63 | convolution fusion | flops 1744830464 | bytes 9568256 | tf_op jit(solution)/shard_map/dot_general | solution.py:175
  17.1 1.7 pad_maximum_fusion.2
  18.8 0.0 reduce-scatter.3.cloned.1.call-update
  18.8 0.2 all-gather.2.cloned.1.call-start
  19.1 17.9 %fusion.34 = f32[1024,512]{0,1:T(8,128)} fusion(s32[1,3328,512]{2,1,0:T(8,128)} %param.7, bf16[1,3328,1024]{2,1,0:T(8,128)(2,1)} %param.6), kind=kOutput, calls=%fused_computation.66 | convolution fusion | flops 3568041984 | bytes 15728640 | tf_op jit(solution)/shard_map/dot_general | solution.py:175
  36.9 1.9 %copy.24 = f32[1024,512]{1,0:T(8,128)S(1)} copy(f32[1024,512]{0,1:T(8,128)} %fusion.34) | data formatting | bytes 4194304 | tf_op jit(solution)/shard_map/dot_general | solution.py:175
  38.8 1.6 copy.25
  40.4 18.4 %fusion.31 = f32[1024,512]{0,1:T(8,128)} fusion(s32[1,3328,512]{2,1,0:T(8,128)} %param.7, bf16[1,3328,1024]{2,1,0:T(8,128)(2,1)} %param.6), kind=kOutput, calls=%fused_computation.65 | convolution fusion | flops 3569745920 | bytes 15728640 | tf_op jit(solution)/shard_map/dot_general | solution.py:175
  58.8 1.9 %copy.22 = f32[1024,512]{1,0:T(8,128)S(1)} copy(f32[1024,512]{0,1:T(8,128)} %fusion.31) | data formatting | bytes 4194304 | tf_op jit(solution)/shard_map/dot_general | solution.py:175
  60.7 0.0 copy-start.3
  60.8 0.2 copy.23
  61.0 1.4 copy-done.3
  62.3 0.0 copy-start.4
  62.3 2.4 %pad_maximum_fusion = f32[1024,1024]{1,0:T(8,128)} fusion(f32[1024,512]{1,0:T(8,128)S(1)} %bitcast.75, f32[1024,512]{1,0:T(8,128)S(1)} %bitcast.76), kind=kLoop, calls=%fused_computation.23 | loop fusion | flops 1048576 | bytes 8388608 | tf_op jit(solution)/shard_map/concatenate | solution.py:253
  64.8 0.5 reduce-scatter.3.cloned.1.call-done
  65.2 0.0 all-gather.2.cloned.1.call-update
  65.3 0.0 reduce-scatter.5.cloned.1.call-start
  66.0 0.0 copy-done.4
  66.0 3.9 %negate_select_fusion.6 = (f32[1024,512]{1,0:T(8,128)S(1)}, f32[1024,512]{1,0:T(8,128)S(1)}) fusion(s32[1,1024,512]{2,1,0:T(8,128)S(1)} %copy-done.4), kind=kLoop, calls=%fused_computation.37 | loop fusion | flops 26738688 | bytes 6291456 | tf_op jit(solution)/shard_map/jit(_where)/select_n | solution.py:191
  69.9 0.0 copy-start.5
  69.9 0.0 copy-start.6
  69.9 2.4 %pad_maximum_fusion.1 = f32[1024,1024]{1,0:T(8,128)} fusion(f32[1024,512]{1,0:T(8,128)S(1)} %get-tuple-element.20, f32[1024,512]{1,0:T(8,128)S(1)} %get-tuple-element.19), kind=kLoop, calls=%fused_computation.24 | loop fusion | flops 1048576 | bytes 8388608 | tf_op jit(solution)/shard_map/concatenate | solution.py:255
  72.3 0.0 copy-done.5
  72.3 0.0 copy-done.6
  72.3 5.9 %select_add_fusion.coh_ref = f32[1024,1024]{1,0:T(8,128)} fusion(f32[1024]{0:T(1024)S(1)} %bitcast.79, f32[1024]{0:T(1024)S(1)} %fusion.42, f32[1024]{0:T(1024)S(1)} %get-tuple-element.24, f32[]{:T(128)} %bitcast.12, f32[1024]{0:T(1024)S(1)} %bitcast.80, s32[1024]{0:T(1024)S(1)} %get-tuple-element.23), kind=kLoop, calls=%fused_computation.25 | loop fusion | flops 14680064 | bytes 4214788 | tf_op jit(solution)/shard_map/add | solution.py:171
  78.2 19.5 %all-gather.2.cloned.1.call-done.sum_ref = f32[2560,256]{1,0:T(8,128)} async-done(((f32[320,256]{1,0:T(8,128)}), f32[2560,256]{1,0:T(8,128)}) %all-gather.2.cloned.1.call-update) | async-done | bytes 2621456 | tf_op jit(solution)/shard_map/all_gather | solution.py:257
  97.7 0.0 copy-start
  97.7 0.0 reduce-scatter.5.cloned.1.call-update
  97.7 1.7 copy-done
  99.4 0.0 copy-start.1
  99.4 2.2 %copy-done.1 = f32[1024,1024]{1,0:T(8,128)S(1)} copy-done((f32[1024,1024]{1,0:T(8,128)S(1)}, f32[1024,1024]{1,0:T(8,128)}, u32[]{:S(2)}) %copy-start.1) | copy-done | bytes 4194328
  101.6 44.4 %factor.1 = f32[1024,1024]{1,0:T(8,128)S(1)} custom-call(f32[1024,1024]{1,0:T(8,128)S(1)} %copy-done.1, f32[2560,256]{1,0:T(8,128)S(1)} %copy-done), custom_call_target="tpu_custom_call" | custom-call | flops 40000000000 | bytes 11534336 | tf_op jit(solution)/shard_map/factor/pallas_call | solution.py:125
  146.1 6.1 %reduce-scatter.5.cloned.1.call-done = f32[128,1024]{1,0:T(8,128)} async-done(((f32[1024,1024]{1,0:T(8,128)}), f32[128,1024]{1,0:T(8,128)}) %reduce-scatter.5.cloned.1.call-update) | async-done | bytes 524304 | tf_op jit(solution)/shard_map/reduce_scatter | solution.py:261
  152.2 3.7 %fusion.37 = f32[1024,128]{0,1:T(8,128)S(1)} fusion(f32[128,1024]{1,0:T(8,128)} %reduce-scatter.5.cloned.1.call-done, f32[1024,1024]{1,0:T(8,128)} %pad_maximum_fusion.1, f32[64,1024]{1,0:T(8,128)S(1)} %get-tuple-element.18, f32[64,1024]{1,0:T(8,128)S(1)} %get-tuple-element.17), kind=kOutput, calls=%fused_computation.68 | convolution fusion | flops 805568512 | bytes 5767168 | tf_op jit(solution)/shard_map/dot_general | solution.py:271
  155.9 0.4 reshape.202
  156.3 1.1 copy.26
  157.4 4.6 %all-to-all-start = ((f32[2,512,128]{2,0,1:T(2,128)}), f32[2,512,128]{2,0,1:T(2,128)S(1)}, u32[]{:S(2)}, u32[]{:S(2)}) async-start(f32[2,512,128]{2,0,1:T(2,128)} %copy.26), calls=%async_computation.2 | async-start | bytes 1048576 | tf_op jit(solution)/shard_map/all_to_all | solution.py:273
  162.0 0.1 fusion.52
  162.2 14.2 %all-to-all-done = f32[2,512,128]{2,0,1:T(2,128)S(1)} async-done(((f32[2,512,128]{2,0,1:T(2,128)}), f32[2,512,128]{2,0,1:T(2,128)S(1)}, u32[]{:S(2)}, u32[]{:S(2)}) %all-to-all-start) | async-done | bytes 524320 | tf_op jit(solution)/shard_map/all_to_all | solution.py:273
  176.4 0.3 copy.32
  176.8 7.9 %synth.1 = f32[16384,256]{1,0:T(8,128)} custom-call(f32[8,16384]{1,0:T(8,128)S(1)} %bitcast.68, f32[8,256]{1,0:T(8,128)S(1)} %reshape.204.table_ref), custom_call_target="tpu_custom_call" | custom-call | tf_op jit(solution)/shard_map/synth/pallas_call | solution.py:219
  (9 shorter events, 0.2 us)
Async XLA Ops:
  6.5 58.7 %reduce-scatter.3.cloned.1.call-start = ((), (), s32[]{:S(2)}) async-start(), calls=%async_computation.3 | async-start | bytes 2949120 | tf_op jit(solution)/shard_map/reduce_scatter | solution.py:246
  9.2 4.5 %copy-start.2 = (bf16[1,3328,1024]{2,1,0:T(8,128)(2,1)S(1)}, bf16[1,3328,1024]{2,1,0:T(8,128)(2,1)}, u32[]{:S(2)}) copy-start(bf16[1,3328,1024]{2,1,0:T(8,128)(2,1)} %param.6) | copy-start | bytes 20447236
  18.8 78.8 %all-gather.2.cloned.1.call-start = ((), (), s32[]{:S(2)}) async-start(), calls=%async_computation.4 | async-start | bytes 2949120 | tf_op jit(solution)/shard_map/all_gather | solution.py:257
  60.7 1.6 copy-start.3
  62.3 3.6 %copy-start.4 = (s32[1,1024,512]{2,1,0:T(8,128)S(1)}, s32[1,1024,512]{2,1,0:T(8,128)}, u32[]{:S(2)}) copy-start(s32[1,1024,512]{2,1,0:T(8,128)} %param.8) | copy-start | bytes 6291460
  65.3 87.0 %reduce-scatter.5.cloned.1.call-start = ((), (), s32[]{:S(2)}) async-start(), calls=%async_computation.5 | async-start | bytes 4718592 | tf_op jit(solution)/shard_map/reduce_scatter | solution.py:261
  69.9 2.4 %copy-start.5 = (f32[1,1024]{1,0:T(1,128)S(1)}, f32[1,1024]{1,0:T(1,128)}, u32[]{:S(2)}) copy-start(f32[1,1024]{1,0:T(1,128)} %param.10) | copy-start | bytes 12292
  69.9 2.4 %copy-start.6 = (f32[1,1024]{1,0:T(1,128)S(1)}, f32[1,1024]{1,0:T(1,128)}, u32[]{:S(2)}) copy-start(f32[1,1024]{1,0:T(1,128)} %param.9) | copy-start | bytes 12292
  97.7 1.7 copy-start
  99.4 2.2 %copy-start.1 = (f32[1024,1024]{1,0:T(8,128)S(1)}, f32[1024,1024]{1,0:T(8,128)}, u32[]{:S(2)}) copy-start(f32[1024,1024]{1,0:T(8,128)} %select_add_fusion.coh_ref) | copy-start | bytes 12582916
  157.4 18.9 %all-to-all-start = ((f32[2,512,128]{2,0,1:T(2,128)}), f32[2,512,128]{2,0,1:T(2,128)S(1)}, u32[]{:S(2)}, u32[]{:S(2)}) async-start(f32[2,512,128]{2,0,1:T(2,128)} %copy.26), calls=%async_computation.2 | async-start | bytes 1048576 | tf_op jit(solution)/shard_map/all_to_all | solution.py:273
Sparse Core Ops, SparseCore 0:
  19.0 46.2 reduce-scatter.2
  67.1 30.5 all-gather.1
  101.0 51.1 reduce-scatter.4

commit v3 on v2

--- a/solution.py
+++ b/solution.py
@@ -193,6 +193,137 @@
     )
 
 
+def quick_waves(seeds):
+    quarter = NPHASE // 4
+    turn = (seeds + quarter // 2) >> (quarter.bit_length() - 1)
+    x = (seeds - turn * quarter).astype(jnp.float32) * (2.0 * math.pi / NPHASE)
+    y = x * x
+    sin = x * (1.0 + y * (-1 / 6 + y * (1 / 120 + y * (-1 / 5040 + y * (1 / 362880)))))
+    cos = 1.0 + y * (-1 / 2 + y * (1 / 24 + y * (-1 / 720 + y * (1 / 40320))))
+    odd = (turn & 1) == 1
+    re = jnp.where(odd, sin, cos)
+    im = jnp.where(odd, cos, sin)
+    return (
+        jnp.where(((turn + 1) & 2) == 2, -re, re),
+        jnp.where((turn & 2) == 2, -im, im),
+    )
+
+
+def reduce_kernel(
+    parts, n_col, packed_ref, cols_ref, seeds_ref, out_ref, prod_ref, sum_ref, land_ref, send_sem,
+    recv_sem,
+):
+    me = lax.axis_index("row") * n_col + lax.axis_index("col")
+    stages = parts.bit_length() - 1
+    core = me % 2
+    upper = [2**s for s in range(1, stages)]
+    turned = upper[1:] + upper[:1]
+    bits = [1] + [a + core * (b - a) for a, b in zip(upper, turned)]
+
+    def partner(bit):
+        other = me + bit * (1 - 2 * ((me // bit) % 2))
+        return {"row": other // n_col, "col": other % n_col}
+
+    barrier = pltpu.get_barrier_semaphore()
+    for bit in bits:
+        pl.semaphore_signal(
+            barrier, inc=1, device_id=partner(bit), device_id_type=pl.DeviceIdType.MESH
+        )
+    pl.semaphore_wait(barrier, stages)
+
+    depth, window = cols_ref.shape
+    seed_count = seeds_ref.shape[1]
+    own = prod_ref.shape[2]
+    tall = 256
+    chunk = next(c for c in (256, 208, 128, 64, 32, 16) if depth % c == 0)
+    chunks = depth // chunk
+
+    def products(first, last):
+        @pl.loop(first, last)
+        def _(step):
+            at = pl.ds(pl.multiple_of(step * chunk, chunk), chunk)
+            wave_re, wave_im = quick_waves(seeds_ref[at, :])
+            waves = jnp.concatenate(
+                [wave_re.astype(jnp.bfloat16), wave_im.astype(jnp.bfloat16)], axis=1
+            )
+            for r in range(window // tall):
+                term = lax.dot_general(
+                    cols_ref[at, r * tall:(r + 1) * tall],
+                    waves,
+                    (((0,), (0,)), ((), ())),
+                    preferred_element_type=jnp.float32,
+                ).reshape(tall // own, own, 2 * seed_count)
+                half, base = divmod(r * tall, window // 2)
+                there = slice(base // own, base // own + tall // own)
+                prod_ref[there, half] += term
+
+    share = [chunks * i // (2 * stages) for i in range(2 * stages + 1)]
+    kept = []
+    start, size, slot = 0, packed_ref.shape[0], 0
+    for s, bit in enumerate(bits):
+        size //= 2
+        mine = (me // bit) % 2
+        keep = pl.ds(pl.multiple_of(start + mine * size, 8), size)
+        give = pl.ds(pl.multiple_of(start + (1 - mine) * size, 8), size)
+        source = packed_ref if s == 0 else sum_ref
+        landed = pl.ds(slot, size)
+        copy = pltpu.make_async_remote_copy(
+            src_ref=source.at[give],
+            dst_ref=land_ref.at[landed],
+            send_sem=send_sem.at[s],
+            recv_sem=recv_sem.at[s],
+            device_id=partner(bit),
+            device_id_type=pl.DeviceIdType.MESH,
+        )
+        copy.start()
+        if s == 0:
+            prod_ref[...] = jnp.zeros_like(prod_ref)
+        products(share[s], share[s + 1])
+        copy.wait()
+        total_ref = out_ref if s == stages - 1 else sum_ref
+        total_ref[keep, :] = source[keep, :] + land_ref[landed, :]
+        kept.append(keep)
+        start = start + mine * size
+        slot += size
+    for back, s in enumerate(reversed(range(stages))):
+        copy = pltpu.make_async_remote_copy(
+            src_ref=out_ref.at[kept[s]],
+            dst_ref=out_ref.at[kept[s]],
+            send_sem=send_sem.at[stages + back],
+            recv_sem=recv_sem.at[stages + back],
+            device_id=partner(bits[s]),
+            device_id_type=pl.DeviceIdType.MESH,
+        )
+        copy.start()
+        products(share[stages + back], share[stages + back + 1])
+        copy.wait()
+
+
+def reduce_and_multiply(packed, cols, seeds, parts, n_col):
+    window = cols.shape[1]
+    quarter = window // (2 * parts)
+    stages = parts.bit_length() - 1
+    return pl.pallas_call(
+        functools.partial(reduce_kernel, parts, n_col),
+        name="reduce",
+        out_shape=(
+            jax.ShapeDtypeStruct(packed.shape, jnp.float32),
+            jax.ShapeDtypeStruct((parts, 2, quarter, 2 * seeds.shape[1]), jnp.float32),
+        ),
+        in_specs=[pl.BlockSpec(memory_space=pltpu.VMEM)] * 3,
+        out_specs=[pl.BlockSpec(memory_space=pltpu.VMEM)] * 2,
+        scratch_shapes=[
+            pltpu.VMEM(packed.shape, jnp.float32),
+            pltpu.VMEM(packed.shape, jnp.float32),
+            pltpu.SemaphoreType.DMA((2 * stages,)),
+            pltpu.SemaphoreType.DMA((2 * stages,)),
+        ],
+        compiler_params=pltpu.CompilerParams(
+            collective_id=0, has_side_effects=True, vmem_limit_bytes=48 * 2**20
+        ),
+    )(packed, cols, seeds)
+
+
 def synth_kernel(x_ref, table_ref, out_ref):
     def parts(value):
         high = value.astype(jnp.bfloat16).astype(jnp.float32)
@@ -243,21 +374,10 @@
     packed = jnp.concatenate(
         [against(cols[:, at:], cols[:, at:at + wide]) for at in range(0, window, wide)], axis=0
     )
-    packed = lax.psum_scatter(packed, AXES, scatter_dimension=0, tiled=True)
-
-    def stored(wave):
-        whole = against(cols, wave.astype(jnp.bfloat16)).reshape(2, parts, quarter, seed_count)
-        return jnp.transpose(whole, (1, 0, 2, 3)).reshape(window, seed_count)
-
-    wave_re, wave_im = waves_of(prior_seeds[0])
-    whole = jnp.concatenate([stored(wave_re), stored(wave_im)], axis=1)
     coh = coherence(spectra[0], nugget[0], decay[0])
     window_waves = jnp.concatenate(waves_of(window_seeds[0]), axis=1)
-    packed, whole = lax.optimization_barrier((packed, whole))
-    packed = lax.all_gather(packed, AXES, axis=0, tiled=True)
-    packed, whole, coh, window_waves = lax.optimization_barrier(
-        (packed, whole, coh, window_waves)
-    )
+    packed, whole = reduce_and_multiply(packed, cols, prior_seeds[0], parts, lax.axis_size("col"))
+    whole = whole.reshape(window, 2 * seed_count)
     prior = lax.psum_scatter(whole, AXES, scatter_dimension=0, tiled=True)
 
     factor = cholesky(coh, packed)

time: 192 us -> 158 us (0.82)
  Pallas kernels: 52.3 us -> 101 us
  matrix products: 49.7 us -> 12.9 us
  waiting for transfers between devices: 40.3 us -> 13.2 us
  local copies, waits for them, and re-layouts: 13.6 us -> 2.75 us
  other arithmetic: 16.4 us -> 8.85 us
    pallas_call x0 -> x1, Pallas kernels: none -> 48.9 us  [reduce_and_multiply(): pl.pallas_call(functools.partial(reduce_kernel, parts, n_col), name='redu...]
    dot_general x6 -> x4, matrix products: 46.1 us -> 9.81 us  [against(): lax.dot_general(picked, other, (((0,), (0,)), ((), ())), preferred_elemen...]
    all_gather x1 -> x0, waiting for transfers between devices: 19.5 us -> none  [shards(): packed = lax.all_gather(packed, AXES, axis=0, tiled=True)]
    reduce_scatter x1, waiting for transfers between devices: 6.13 us -> 0.01 us  [shards(): prior = lax.psum_scatter(whole, AXES, scatter_dimension=0, tiled=True)]
    unnamed x15 -> x9, local copies, waits for them, and re-layouts: 6.34 us -> 1.09 us
    concatenate x2 -> x0, other arithmetic: 4.8 us -> none  [the longest x1 2.42 us: shards(): whole = jnp.concatenate([stored(wave_re), stored(wave_im)], axis=1)]
    dot_general x2 -> x0, local copies, waits for them, and re-layouts: 3.84 us -> none  [against(): lax.dot_general(picked, other, (((0,), (0,)), ((), ())), preferred_elemen...]
    add x1, other arithmetic: 5.86 us -> 3.9 us  [coherence(): return coupling * amplitude * jnp.exp(-decay * distance) + diagonal]
  transfers between devices with their start and end apart: 4 -> 2, of which waited for: 4 -> 1; matrix products, arithmetic and copies ran while one was open for 30% -> 6% of each run, Pallas kernels for 23% -> 28%
where the time goes in v3:
time: 158 us
  Pallas kernels  101 us (64%)
  between operations  14.2 us (9%)
  waiting for transfers between devices  13.2 us (8%)
  matrix products  12.9 us (8%)
  other arithmetic  8.85 us (6%)
  starting transfers between devices  4.87 us (3%)
  local copies, waits for them, and re-layouts  2.75 us (2%)
    pallas_call x1, Pallas kernels, reduce_and_multiply(): pl.pallas_call(functools.partial(reduce_kernel, parts, n_col), name='redu...  48.9 us
    pallas_call x1, Pallas kernels, cholesky(): pl.pallas_call(chol_kernel, name='factor', out_shape=jax.ShapeDtypeStruct...  44.5 us
    all_to_all x1, waiting for transfers between devices, shards(): lax.all_to_all(turned, 'freq', split_axis=1, concat_axis=0, tiled=True)  13.2 us
    dot_general x4, matrix products, against(): lax.dot_general(picked, other, (((0,), (0,)), ((), ())), preferred_elemen...  9.81 us
    pallas_call x1, Pallas kernels, synthesize(): pl.pallas_call(synth_kernel, name='synth', grid=(count // step,), out_sha...  7.9 us
    all_to_all x1, starting transfers between devices, shards(): lax.all_to_all(turned, 'freq', split_axis=1, concat_axis=0, tiled=True)  4.87 us
    select_n x1, other arithmetic, waves_of(): jnp.where(turn + 1 & 2 == 2, -re, re)  4.61 us
    add x1, other arithmetic, coherence(): return coupling * amplitude * jnp.exp(-decay * distance) + diagonal  3.9 us
  transfers between devices with their start and end apart: 2, of which 1 were waited for; matrix products, arithmetic and copies ran while one was open for 6% of the time, Pallas kernels for 28%

profile of v3, /device:TPU:0, one launch (start us, length us, event | category | flops | bytes accessed | tf_op | source)
XLA Modules:
  0.0 158.1 jit_solution(9014416261415182471)
XLA Ops:
  6.5 0.0 reduce-scatter.2.cloned.1.call-start
  6.5 2.6 %fusion.14 = f32[256,256]{1,0:T(8,128)S(1)} fusion(bf16[3328,1024]{1,0:T(8,128)(2,1)} %bitcast.44), kind=kOutput, calls=%fused_computation.33 | convolution fusion | flops 436207616 | bytes 1966080 | tf_op jit(solution)/shard_map/dot_general | solution.py:175
  9.2 0.0 copy-start
  9.2 3.7 %fusion.6 = f32[512,256]{1,0:T(8,128)S(1)} fusion(bf16[3328,1024]{1,0:T(8,128)(2,1)} %bitcast.45), kind=kOutput, calls=%fused_computation.8 | convolution fusion | flops 872415232 | bytes 5636096 | tf_op jit(solution)/shard_map/dot_general | solution.py:175
  12.9 0.8 copy-done
  13.6 1.5 fusion
  15.2 2.0 %fusion.18 = f32[1024,256]{1,0:T(8,128)S(1)} fusion(bf16[3328,1024]{1,0:T(8,128)(2,1)S(1)} %bitcast.48), kind=kOutput, calls=%fused_computation.37 | convolution fusion | flops 1744830464 | bytes 9568256 | tf_op jit(solution)/shard_map/dot_general | solution.py:175
  17.1 0.2 pad_maximum_fusion.packed_ref
  17.3 48.9 %reduce.1 = (f32[2560,256]{1,0:T(8,128)S(1)}, f32[8,2,64,1024]{3,2,1,0:T(8,128)}) custom-call(f32[2560,256]{1,0:T(8,128)S(1)} %pad_maximum_fusion.packed_ref, bf16[3328,1024]{1,0:T(8,128)(2,1)} %bitcast.46, s32[3328,512]{1,0:T(8,128)} %bitcast.49), custom_call_target="tpu_custom_call" | custom-call | tf_op jit(solution)/shard_map/reduce/pallas_call | solution.py:306
  66.3 0.0 copy-start.2
  66.3 0.0 copy-start.3
  66.3 0.0 reduce-scatter.2.cloned.1.call-update
  67.0 0.0 copy-done.2
  67.0 0.0 copy-done.3
  67.0 3.9 %select_add_fusion.coh_ref = f32[1024,1024]{1,0:T(8,128)S(1)} fusion(f32[1024]{0:T(1024)S(1)} %bitcast.53, f32[1024]{0:T(1024)S(1)} %fusion.30, f32[1024]{0:T(1024)S(1)} %get-tuple-element.16, f32[]{:T(128)} %bitcast.4, f32[1024]{0:T(1024)S(1)} %bitcast.54, s32[1024]{0:T(1024)S(1)} %get-tuple-element.15), kind=kLoop, calls=%fused_computation.6 | loop fusion | flops 14680064 | bytes 4214788 | tf_op jit(solution)/shard_map/add | solution.py:171
  70.9 0.0 copy-start.1
  71.0 44.5 %factor.1 = f32[1024,1024]{1,0:T(8,128)S(1)} custom-call(f32[1024,1024]{1,0:T(8,128)S(1)} %select_add_fusion.coh_ref, f32[2560,256]{1,0:T(8,128)S(1)} %get-tuple-element.8.sum_ref), custom_call_target="tpu_custom_call" | custom-call | flops 40000000000 | bytes 11534336 | tf_op jit(solution)/shard_map/factor/pallas_call | solution.py:125
  115.5 0.0 copy-done.1
  115.5 4.6 %negate_select_fusion.1 = (f32[1024,512]{1,0:T(8,128)S(1)}, f32[1024,512]{1,0:T(8,128)}) fusion(s32[1,1024,512]{2,1,0:T(8,128)S(1)} %copy-done.1), kind=kLoop, calls=%fused_computation.11 | loop fusion | flops 26738688 | bytes 6291456 | tf_op jit(solution)/shard_map/jit(_where)/select_n | solution.py:191
  120.1 0.0 reduce-scatter.2.cloned.1.call-done
  120.1 3.1 %fusion.23 = f32[1024,128]{0,1:T(8,128)S(1)} fusion(f32[128,1024]{1,0:T(8,128)} %reduce-scatter.2.cloned.1.call-done, f32[1024,512]{1,0:T(8,128)} %get-tuple-element.12, f32[1024,512]{1,0:T(8,128)S(1)} %get-tuple-element.11, f32[64,1024]{1,0:T(8,128)S(1)} %get-tuple-element.10, f32[64,1024]{1,0:T(8,128)S(1)} %get-tuple-element.9), kind=kOutput, calls=%fused_computation.40 | convolution fusion | flops 806617088 | bytes 5767168 | tf_op jit(solution)/shard_map/dot_general | solution.py:391
  123.2 0.4 reshape.188
  123.6 1.1 copy.12
  124.7 4.9 %all-to-all-start = ((f32[2,512,128]{2,0,1:T(2,128)}), f32[2,512,128]{2,0,1:T(2,128)S(1)}, u32[]{:S(2)}, u32[]{:S(2)}) async-start(f32[2,512,128]{2,0,1:T(2,128)} %copy.12), calls=%async_computation.1 | async-start | bytes 1048576 | tf_op jit(solution)/shard_map/all_to_all | solution.py:393
  129.6 0.1 fusion.40
  129.8 13.2 %all-to-all-done = f32[2,512,128]{2,0,1:T(2,128)S(1)} async-done(((f32[2,512,128]{2,0,1:T(2,128)}), f32[2,512,128]{2,0,1:T(2,128)S(1)}, u32[]{:S(2)}, u32[]{:S(2)}) %all-to-all-start) | async-done | bytes 524320 | tf_op jit(solution)/shard_map/all_to_all | solution.py:393
  143.0 0.3 copy.18
  143.3 7.9 %synth.1 = f32[16384,256]{1,0:T(8,128)} custom-call(f32[8,16384]{1,0:T(8,128)S(1)} %bitcast.43, f32[8,256]{1,0:T(8,128)S(1)} %reshape.190.table_ref), custom_call_target="tpu_custom_call" | custom-call | tf_op jit(solution)/shard_map/synth/pallas_call | solution.py:350
  (9 shorter events, 0.2 us)
Async XLA Ops:
  6.5 113.6 %reduce-scatter.2.cloned.1.call-start = ((), (), s32[]{:S(2)}) async-start(), calls=%async_computation.2 | async-start | bytes 4718592 | tf_op jit(solution)/shard_map/reduce_scatter | solution.py:381
  9.2 4.5 %copy-start = (bf16[1,3328,1024]{2,1,0:T(8,128)(2,1)S(1)}, bf16[1,3328,1024]{2,1,0:T(8,128)(2,1)}, u32[]{:S(2)}) copy-start(bf16[1,3328,1024]{2,1,0:T(8,128)(2,1)} %param.6) | copy-start | bytes 20447236
  66.3 0.7 copy-start.2
  66.3 0.7 copy-start.3
  70.9 44.5 %copy-start.1 = (s32[1,1024,512]{2,1,0:T(8,128)S(1)}, s32[1,1024,512]{2,1,0:T(8,128)}, u32[]{:S(2)}) copy-start(s32[1,1024,512]{2,1,0:T(8,128)} %param.8) | copy-start | bytes 6291460
  124.7 18.2 %all-to-all-start = ((f32[2,512,128]{2,0,1:T(2,128)}), f32[2,512,128]{2,0,1:T(2,128)S(1)}, u32[]{:S(2)}, u32[]{:S(2)}) async-start(f32[2,512,128]{2,0,1:T(2,128)} %copy.12), calls=%async_computation.1 | async-start | bytes 1048576 | tf_op jit(solution)/shard_map/all_to_all | solution.py:393
Sparse Core Ops, SparseCore 0:
  66.4 52.0 reduce-scatter.1
